TPU v7x, 32 devices: a whole 2x2x4 slice. The times are simulated.
32 devices in a mesh: ctx: 4 (over z), head: 8 (over y, x, core).
Axes of the slice: x: 2, y: 2, z: 4, core: 2. Of those that a mesh axis runs over, the one named last changes fastest.
Arguments:
- hidden: float32 [1024, 2304], P(('ctx', 'head')), may hold values from -40 to 40
- w_query: float32 [2304, 1536], P(None, 'head'), may hold values from -0.125 to 0.125
- w_down: float32 [2304, 576], replicated, may hold values from -0.125 to 0.125
- latent_gain: float32 [512], replicated, may hold values from 0.25 to 1.75
- w_key_up: float32 [512, 1024], P(None, 'head'), may hold values from -0.25 to 0.25
- w_value_up: float32 [512, 1024], P(None, 'head'), may hold values from -0.25 to 0.25
- w_out: float32 [1024, 2304], P('head'), may hold values from -0.1875 to 0.1875
Outputs:
- output: float32 [1024, 2304], P(('ctx', 'head'))
All inputs are finite; a program needn't handle non-finite values.
Results may differ from a plain program's by a relative error of at most 0.0003.
Values sent between devices are 32-bit elements; how exact they have to be, the bound alone decides.
A program may use at most 64 MiB of HBM per device.

v0:
```python
import jax
import jax.numpy as jnp
from jax import lax
from jax.sharding import PartitionSpec as P

EXACT = lax.Precision.HIGHEST
EPSILON = 1e-06
FLOOR = -1e30


def matmul(left, right):
    return jnp.dot(left, right, precision=EXACT, preferred_element_type=jnp.float32)


def on_device(hidden, w_query, w_down, latent_gain, w_key_up, w_value_up, w_out):
    rank = w_key_up.shape[0]
    nope = w_key_up.shape[1]
    down_part = matmul(hidden, w_down)
    raw_latent = down_part[:, :rank]
    meansq = jnp.mean(raw_latent * raw_latent, axis=-1, keepdims=True)
    own_latent = jnp.concatenate(
        [raw_latent * lax.rsqrt(meansq + EPSILON) * latent_gain, down_part[:, rank:]], axis=1
    )
    latent_block = lax.all_gather(own_latent, "head", axis=0, tiled=True)
    queries = matmul(lax.all_gather(hidden, "head", axis=0, tiled=True), w_query)
    row_count = queries.shape[0]
    score_scale = queries.shape[1] ** (-0.5)
    query_pos = lax.axis_index("ctx") * row_count + jnp.arange(row_count, dtype=jnp.int32)
    latent_part = latent_block[:, :rank]
    projected = jnp.concatenate(
        [matmul(latent_part, w_key_up), latent_block[:, rank:], matmul(latent_part, w_value_up)],
        axis=1,
    )
    shared_end = nope + latent_block.shape[1] - rank
    portion = lax.all_gather(projected, "ctx", axis=0, tiled=True)
    key_own = portion[:, :nope]
    maxima = jnp.full((row_count,), FLOOR, jnp.float32)
    scores = (
        matmul(queries[:, :nope], key_own.T)
        + matmul(queries[:, nope:], portion[:, nope:shared_end].T)
    ) * score_scale
    key_pos = jnp.arange(key_own.shape[0], dtype=jnp.int32)
    causal = query_pos[:, None] >= key_pos[None, :]
    scores = jnp.where(causal, scores, FLOOR)
    new_max = jnp.maximum(maxima, jnp.max(scores, axis=1))
    weights = jnp.where(causal, jnp.exp(scores - new_max[:, None]), 0.0)
    attended = matmul(weights, portion[:, shared_end:]) / jnp.sum(weights, axis=1)[:, None]
    return lax.psum_scatter(matmul(attended, w_out), "head", scatter_dimension=0, tiled=True)


def solution(mesh):
    placed = (
        P(("ctx", "head"), None),
        P(None, "head"),
        P(),
        P(),
        P(None, "head"),
        P(None, "head"),
        P("head", None),
    )
    return jax.shard_map(
        on_device, mesh=mesh, in_specs=placed, out_specs=P(("ctx", "head"), None), check_vma=False
    )
```

profile of v0, /device:TPU:0, one launch (start us, length us, event | category | flops | bytes accessed | tf_op | source)
XLA Modules:
  0.0 135.4 jit_solution(8996285080578068677)
XLA Ops:
  6.5 0.7 all-gather.3.cloned.1.call-update
  7.3 0.0 all-gather.5.cloned.1.call-start
  7.3 7.2 %fusion.19 = f32[32,576]{1,0:T(8,128)S(1)} fusion(f32[32,2304]{1,0:T(8,128)} %param.7, f32[2304,576]{0,1:T(8,128)} %param.9), kind=kOutput, calls=%fused_computation.30 | convolution fusion | flops 509607936 | bytes 5677056 | tf_op jit(solution)/shard_map/dot_general | solution.py:12
  14.5 0.0 copy-start.2
  14.5 0.0 copy-start.3
  14.5 0.1 multiply_reduce_fusion
  14.6 0.1 multiply_multiply_fusion
  14.7 13.6 %all_gather.10 = f32[256,576]{1,0:T(8,128)S(1)} all-gather(f32[32,576]{1,0:T(8,128)S(1)} %pad_maximum_fusion.1), channel_id=1, replica_groups=mesh['ctx'=4,'head'=8] {'head'}, dimensions={0}, use_global_device_ids=true | all-gather | bytes 663552 | tf_op jit(solution)/shard_map/all_gather | solution.py:24
  28.3 0.1 copy.8
  28.4 0.6 fusion.8
  29.0 0.6 fusion.10
  29.6 0.7 pad_maximum_fusion
  30.4 0.0 all-gather.5.cloned.1.call-update
  30.4 0.2 reduce-scatter.2.cloned.1.call-start
  30.6 12.1 %all-gather.3.cloned.1.call-done = f32[256,2304]{1,0:T(8,128)} async-done(((f32[32,2304]{1,0:T(8,128)}), f32[256,2304]{1,0:T(8,128)}) %all-gather.3.cloned.1.call-update) | async-done | bytes 2359312 | tf_op jit(solution)/shard_map/all_gather | solution.py:25
  42.7 4.1 %fusion.18 = f32[256,192]{0,1:T(8,128)S(1)} fusion(f32[256,2304]{1,0:T(8,128)} %all-gather.3.cloned.1.call-done, f32[2304,192]{0,1:T(8,128)S(1)} %copy-done), kind=kOutput, calls=%fused_computation.29 | convolution fusion | flops 1358954496 | bytes 4325376 | tf_op jit(solution)/shard_map/dot_general | solution.py:12
  46.9 30.0 %all-gather.5.cloned.1.call-done = f32[1024,320]{0,1:T(8,128)} async-done(((f32[256,320]{0,1:T(8,128)}), f32[1024,320]{0,1:T(8,128)}) %all-gather.5.cloned.1.call-update) | async-done | bytes 1310736 | tf_op jit(solution)/shard_map/all_gather | solution.py:35
  76.9 2.0 %fusion.12 = f32[256,1024]{1,0:T(8,128)S(1)} fusion(f32[1024,320]{0,1:T(8,128)} %all-gather.5.cloned.1.call-done, f32[256,192]{0,1:T(8,128)S(1)} %fusion.18), kind=kOutput, calls=%fused_computation.17 | convolution fusion | flops 201326592 | bytes 1376256 | tf_op jit(solution)/shard_map/dot_general | solution.py:12
  78.8 2.3 %fusion.17 = (f32[256]{0:T(256)S(1)}, f32[256,1024]{1,0:T(8,128)S(1)}) fusion(f32[256,1024]{1,0:T(8,128)S(1)} %fusion.12, f32[1024,320]{0,1:T(8,128)} %all-gather.5.cloned.1.call-done, f32[256,192]{0,1:T(8,128)S(1)} %fusion.18, s32[256]{0:T(256)S(1)} %iota_add_fusion), kind=kOutput, calls=%fused_computation.28 | convolution fusion | flops 403963648 | bytes 2754560 | tf_op jit(solution)/shard_map/dot_general | solution.py:12
  81.2 0.4 fusion.2
  81.6 2.2 %convolution_divide_fusion = f32[256,128]{1,0:T(8,128)S(1)} fusion(f32[256,1024]{1,0:T(8,128)S(1)} %get-tuple-element.6, f32[1024,320]{0,1:T(8,128)} %all-gather.5.cloned.1.call-done, f32[256]{0:T(256)S(1)} %broadcast_maximum_fusion, s32[256]{0:T(256)S(1)} %iota_add_fusion, f32[256]{0:T(256)S(1)} %fusion.2), kind=kOutput, calls=%fused_computation.3 | convolution fusion | flops 403472384 | bytes 1707008 | tf_op jit(solution)/shard_map/dot_general | solution.py:12
  83.8 3.4 %fusion.20 = f32[256,2304]{1,0:T(8,128)} fusion(f32[256,128]{1,0:T(8,128)S(1)} %convolution_divide_fusion, f32[128,2304]{1,0:T(8,128)S(1)} %copy-done.1), kind=kOutput, calls=%fused_computation.31 | convolution fusion | flops 905969664 | bytes 3670016 | tf_op jit(solution)/shard_map/dot_general | solution.py:12
  87.2 0.0 reduce-scatter.2.cloned.1.call-update
  87.3 41.6 %reduce-scatter.2.cloned.1.call-done = f32[32,2304]{1,0:T(8,128)} async-done(((f32[256,2304]{1,0:T(8,128)}), f32[32,2304]{1,0:T(8,128)}) %reduce-scatter.2.cloned.1.call-update) | async-done | bytes 294928 | tf_op jit(solution)/shard_map/reduce_scatter | solution.py:48
  (15 shorter events, 0.1 us)
Async XLA Ops:
  6.5 36.2 %copy-start = (f32[2304,192]{0,1:T(8,128)S(1)}, f32[2304,192]{0,1:T(8,128)}, u32[]{:S(2)}) copy-start(f32[2304,192]{0,1:T(8,128)} %param.8) | copy-start | bytes 5308420
  6.5 36.2 %all-gather.3.cloned.1.call-start = ((), (), s32[]{:S(2)}) async-start(), calls=%async_computation.1 | async-start | bytes 2654208 | tf_op jit(solution)/shard_map/all_gather | solution.py:25
  7.3 7.4 %copy-start.4 = (f32[512]{0:T(512)S(1)}, f32[512]{0:T(512)}, u32[]{:S(2)}) copy-start(f32[512]{0:T(512)} %param.10) | copy-start | bytes 6148
  7.3 69.6 %all-gather.5.cloned.1.call-start = ((), (), s32[]{:S(2)}) async-start(), calls=%async_computation.2 | async-start | bytes 1638400 | tf_op jit(solution)/shard_map/all_gather | solution.py:35
  14.5 13.9 %copy-start.2 = (f32[512,128]{1,0:T(8,128)S(1)}, f32[512,128]{1,0:T(8,128)}, u32[]{:S(2)}) copy-start(f32[512,128]{1,0:T(8,128)} %param.12) | copy-start | bytes 786436
  14.5 14.5 %copy-start.3 = (f32[512,128]{1,0:T(8,128)S(1)}, f32[512,128]{1,0:T(8,128)}, u32[]{:S(2)}) copy-start(f32[512,128]{1,0:T(8,128)} %param.11) | copy-start | bytes 786436
  30.4 98.5 %reduce-scatter.2.cloned.1.call-start = ((), (), s32[]{:S(2)}) async-start(), calls=%async_computation.3 | async-start | bytes 2654208 | tf_op jit(solution)/shard_map/reduce_scatter | solution.py:48
  81.1 2.6 %copy-start.1 = (f32[128,2304]{1,0:T(8,128)S(1)}, f32[128,2304]{1,0:T(8,128)}, u32[]{:S(2)}) copy-start(f32[128,2304]{1,0:T(8,128)} %param.13) | copy-start | bytes 3538948
Sparse Core Ops, SparseCore 0:
  9.2 33.4 all-gather.2
  44.3 32.5 all-gather.4
  87.4 41.4 reduce-scatter.1
where the time goes:
time: 136 us; the launch traced here: 135 us
  waiting for transfers between devices  84.5 us (62%)
  matrix products  22.4 us (16%)
  blocking collectives  13.6 us (10%)
  between operations  13.3 us (10%)
    reduce_scatter x1, waiting for transfers between devices, on_device(): lax.psum_scatter(matmul(attended, w_out), 'head', scatter_dimension=0, ti...  41.6 us
    all_gather x1, waiting for transfers between devices, on_device(): portion = lax.all_gather(projected, 'ctx', axis=0, tiled=True)  30 us
    dot_general x8, matrix products, matmul(): jnp.dot(left, right, precision=EXACT, preferred_element_type=jnp.float32)  22.4 us
    all_gather x1, blocking collectives, on_device(): latent_block = lax.all_gather(own_latent, 'head', axis=0, tiled=True)  13.6 us
    all_gather x1, waiting for transfers between devices, on_device(): lax.all_gather(hidden, 'head', axis=0, tiled=True)  12.1 us
  transfers between devices with their start and end apart: 3, of which 3 were waited for; matrix products, arithmetic and copies ran while one was open for 10% of the time, Pallas kernels for 0%

commit v1 on v0

--- a/solution.py
+++ b/solution.py
@@ -32,7 +32,12 @@
         axis=1,
     )
     shared_end = nope + latent_block.shape[1] - rank
-    portion = lax.all_gather(projected, "ctx", axis=0, tiled=True)
+    ring = [projected]
+    for hop in range(3):
+        ring.append(lax.ppermute(ring[-1], "ctx", [(dev, (dev + 1) % 4) for dev in range(4)]))
+    portion = jnp.roll(
+        jnp.concatenate(ring[::-1], axis=0), (lax.axis_index("ctx") + 1) * ring[0].shape[0], axis=0
+    )
     key_own = portion[:, :nope]
     maxima = jnp.full((row_count,), FLOOR, jnp.float32)
     scores = (

time: 136 us -> 130 us (0.956)
  waiting for transfers between devices: 84.5 us -> 71.6 us
  local copies, waits for them, and re-layouts: 0.12 us -> 4.94 us
  starting transfers between devices: 0.26 us -> 1.67 us
    ppermute x0 -> x3, waiting for transfers between devices: none -> 31.1 us  [on_device(): lax.ppermute(ring[-1], 'ctx', [(dev, (dev + 1) % 4) for dev in range(4)])]
    all_gather x1 -> x0, waiting for transfers between devices: 30 us -> none  [on_device(): portion = lax.all_gather(projected, 'ctx', axis=0, tiled=True)]
    all_gather x1, waiting for transfers between devices: 12.1 us -> 0.01 us  [on_device(): lax.all_gather(hidden, 'head', axis=0, tiled=True)]
    unnamed x10 -> x16, local copies, waits for them, and re-layouts: 0.02 us -> 4.85 us
    reduce_scatter x1, waiting for transfers between devices: 41.6 us -> 39.7 us  [on_device(): lax.psum_scatter(matmul(attended, w_out), 'head', scatter_dimension=0, ti...]
    ppermute x0 -> x3, starting transfers between devices: none -> 1.63 us  [on_device(): lax.ppermute(ring[-1], 'ctx', [(dev, (dev + 1) % 4) for dev in range(4)])]
  transfers between devices with their start and end apart: 3 -> 5, of which waited for: 3 -> 4; matrix products, arithmetic and copies ran while one was open for 10% -> 12% of each run, Pallas kernels for 0% -> 0%
where the time goes in v1:
time: 130 us
  waiting for transfers between devices  71.6 us (55%)
  matrix products  22.5 us (17%)
  blocking collectives  13.6 us (10%)
  between operations  13.5 us (10%)
  local copies, waits for them, and re-layouts  4.94 us (4%)
  other arithmetic  2.24 us (2%)
  starting transfers between devices  1.67 us (1%)
    reduce_scatter x1, waiting for transfers between devices, on_device(): lax.psum_scatter(matmul(attended, w_out), 'head', scatter_dimension=0, ti...  39.7 us
    ppermute x3, waiting for transfers between devices, on_device(): lax.ppermute(ring[-1], 'ctx', [(dev, (dev + 1) % 4) for dev in range(4)])  31.1 us
    dot_general x8, matrix products, matmul(): jnp.dot(left, right, precision=EXACT, preferred_element_type=jnp.float32)  22.5 us
    all_gather x1, blocking collectives, on_device(): latent_block = lax.all_gather(own_latent, 'head', axis=0, tiled=True)  13.6 us
    unnamed x16, local copies, waits for them, and re-layouts  4.85 us
  transfers between devices with their start and end apart: 5, of which 4 were waited for; matrix products, arithmetic and copies ran while one was open for 12% of the time, Pallas kernels for 0%

profile of v1, /device:TPU:0, one launch (start us, length us, event | category | flops | bytes accessed | tf_op | source)
XLA Modules:
  0.0 130.1 jit_solution(6857529045695230183)
XLA Ops:
  6.5 0.7 all-gather.2.cloned.1.call-update
  7.3 7.2 %fusion.20 = f32[32,576]{1,0:T(8,128)S(1)} fusion(f32[32,2304]{1,0:T(8,128)} %param.7, f32[2304,576]{0,1:T(8,128)} %param.9), kind=kOutput, calls=%fused_computation.39 | convolution fusion | flops 509607936 | bytes 5677056 | tf_op jit(solution)/shard_map/dot_general | solution.py:12
  14.8 13.6 %all_gather.7 = f32[256,576]{1,0:T(8,128)S(1)} all-gather(f32[32,576]{1,0:T(8,128)S(1)} %pad_maximum_fusion.1), channel_id=1, replica_groups=mesh['ctx'=4,'head'=8] {'head'}, dimensions={0}, use_global_device_ids=true | all-gather | bytes 663552 | tf_op jit(solution)/shard_map/all_gather | solution.py:24
  28.4 0.6 fusion.10
  29.0 0.6 fusion.8
  29.7 1.6 %collective-permute-start = (f32[256,320]{0,1:T(8,128)S(1)}, f32[256,320]{0,1:T(8,128)S(1)}, u32[]{:S(2)}, u32[]{:S(2)}) collective-permute-start(f32[256,320]{0,1:T(8,128)S(1)} %pad_maximum_fusion), channel_id=1, source_target_pairs={{0,8},{8,16},{16,24},{24,0},{1,9},{9,17},{17,25},{25,1},{2,10},{10... | collective-permute-start | bytes 983048 | tf_op jit(solution)/shard_map/ppermute | solution.py:37
  31.3 10.2 %collective-permute-done = f32[256,320]{0,1:T(8,128)S(1)} collective-permute-done((f32[256,320]{0,1:T(8,128)S(1)}, f32[256,320]{0,1:T(8,128)S(1)}, u32[]{:S(2)}, u32[]{:S(2)}) %collective-permute-start) | collective-permute-done | bytes 327712 | tf_op jit(solution)/shard_map/ppermute | solution.py:37
  41.5 10.9 %collective-permute-done.1 = f32[256,320]{0,1:T(8,128)S(1)} collective-permute-done((f32[256,320]{0,1:T(8,128)S(1)}, f32[256,320]{0,1:T(8,128)S(1)}, u32[]{:S(2)}, u32[]{:S(2)}) %collective-permute-start.1) | collective-permute-done | bytes 327712 | tf_op jit(solution)/shard_map/ppermute | solution.py:37
  52.4 10.0 %collective-permute-done.2 = f32[256,320]{0,1:T(8,128)S(1)} collective-permute-done((f32[256,320]{0,1:T(8,128)S(1)}, f32[256,320]{0,1:T(8,128)S(1)}, u32[]{:S(2)}, u32[]{:S(2)}) %collective-permute-start.2) | collective-permute-done | bytes 327712 | tf_op jit(solution)/shard_map/ppermute | solution.py:37
  62.5 0.8 constant_dynamic-update-slice_fusion.7
  63.3 0.8 constant_dynamic-update-slice_fusion.6
  64.1 0.8 constant_dynamic-update-slice_fusion.5
  64.9 0.8 constant_dynamic-update-slice_fusion.4
  65.7 0.8 constant_dynamic-update-slice_fusion.3
  66.5 0.8 constant_dynamic-update-slice_fusion.2
  67.3 0.8 constant_dynamic-update-slice_fusion.1
  68.1 0.8 constant_dynamic-update-slice_fusion
  68.9 4.1 %fusion.19 = f32[256,192]{0,1:T(8,128)S(1)} fusion(f32[256,2304]{1,0:T(8,128)} %all-gather.2.cloned.1.call-done, f32[2304,192]{0,1:T(8,128)S(1)} %copy-done), kind=kOutput, calls=%fused_computation.38 | convolution fusion | flops 1358954496 | bytes 4325376 | tf_op jit(solution)/shard_map/dot_general | solution.py:12
  73.0 2.0 %fusion.12 = f32[256,1024]{1,0:T(8,128)S(1)} fusion(f32[2048,320]{0,1:T(8,128)} %constant_dynamic-update-slice_fusion, s32[]{:T(128)S(6)} %select_n.21, s32[]{:T(128)S(6)} %add.47, f32[256,192]{0,1:T(8,128)S(1)} %fusion.19), kind=kOutput, calls=%fused_computation.17 | convolution fusion | flops 201326592 | bytes 1376264 | tf_op jit(solution)/shard_map/dot_general | solution.py:12
  75.0 2.4 %fusion.18 = (f32[256]{0:T(256)S(1)}, f32[256,1024]{1,0:T(8,128)S(1)}) fusion(f32[256,1024]{1,0:T(8,128)S(1)} %fusion.12, f32[2048,320]{0,1:T(8,128)} %constant_dynamic-update-slice_fusion, s32[]{:T(128)S(6)} %select_n.21, f32[256,192]{0,1:T(8,128)S(1)} %fusion.19, s32[256]{0:T(256)S(1)} %iota_add_fusion), kind=kOutput, calls=%fused_computation.37 | convolution fusion | flops 403963648 | bytes 2754564 | tf_op jit(solution)/shard_map/dot_general | solution.py:12
  77.4 0.4 fusion.2
  77.8 2.2 %convolution_divide_fusion = f32[256,128]{1,0:T(8,128)S(1)} fusion(f32[256,1024]{1,0:T(8,128)S(1)} %get-tuple-element.6, f32[2048,320]{0,1:T(8,128)} %constant_dynamic-update-slice_fusion, s32[]{:T(128)S(6)} %select_n.21, s32[]{:T(128)S(6)} %add.48, f32[256]{0:T(256)S(1)} %broadcast_maximum_fusion, s32[256]{0:T(256)S(1)} %iota_add_fusion, f32[256]{0:T(256)S(1)} %fusion.2), kind=kOutput, calls=%fused_computation.3 | convolution fusion | flops 403472384 | bytes 1707016 | tf_op jit(solution)/shard_map/dot_general | solution.py:12
  80.1 3.4 %fusion.21 = f32[256,2304]{1,0:T(8,128)} fusion(f32[256,128]{1,0:T(8,128)S(1)} %convolution_divide_fusion, f32[128,2304]{1,0:T(8,128)S(1)} %copy-done.1), kind=kOutput, calls=%fused_computation.40 | convolution fusion | flops 905969664 | bytes 3670016 | tf_op jit(solution)/shard_map/dot_general | solution.py:12
  83.5 39.7 %reduce-scatter.2.cloned.1.call-done = f32[32,2304]{1,0:T(8,128)} async-done(((f32[256,2304]{1,0:T(8,128)}), f32[32,2304]{1,0:T(8,128)}) %reduce-scatter.2.cloned.1.call-update) | async-done | bytes 294928 | tf_op jit(solution)/shard_map/reduce_scatter | solution.py:53
  (26 shorter events, 0.4 us)
Async XLA Ops:
  6.5 62.4 %copy-start = (f32[2304,192]{0,1:T(8,128)S(1)}, f32[2304,192]{0,1:T(8,128)}, u32[]{:S(2)}) copy-start(f32[2304,192]{0,1:T(8,128)} %param.8) | copy-start | bytes 5308420
  6.5 62.3 %all-gather.2.cloned.1.call-start = ((), (), s32[]{:S(2)}) async-start(), calls=%async_computation.1 | async-start | bytes 2654208 | tf_op jit(solution)/shard_map/all_gather | solution.py:25
  7.3 7.4 %copy-start.4 = (f32[512]{0:T(512)S(1)}, f32[512]{0:T(512)}, u32[]{:S(2)}) copy-start(f32[512]{0:T(512)} %param.10) | copy-start | bytes 6148
  7.3 21.2 %copy-start.2 = (f32[512,128]{1,0:T(8,128)S(1)}, f32[512,128]{1,0:T(8,128)}, u32[]{:S(2)}) copy-start(f32[512,128]{1,0:T(8,128)} %param.11) | copy-start | bytes 786436
  7.3 116.0 %reduce-scatter.2.cloned.1.call-start = ((), (), s32[]{:S(2)}) async-start(), calls=%async_computation.2 | async-start | bytes 2654208 | tf_op jit(solution)/shard_map/reduce_scatter | solution.py:53
  14.5 14.5 %copy-start.3 = (f32[512,128]{1,0:T(8,128)S(1)}, f32[512,128]{1,0:T(8,128)}, u32[]{:S(2)}) copy-start(f32[512,128]{1,0:T(8,128)} %param.12) | copy-start | bytes 786436
  29.7 11.8 %collective-permute-start = (f32[256,320]{0,1:T(8,128)S(1)}, f32[256,320]{0,1:T(8,128)S(1)}, u32[]{:S(2)}, u32[]{:S(2)}) collective-permute-start(f32[256,320]{0,1:T(8,128)S(1)} %pad_maximum_fusion), channel_id=1, source_target_pairs={{0,8},{8,16},{16,24},{24,0},{1,9},{9,17},{17,25},{25,1},{2,10},{10... | collective-permute-start | bytes 983048 | tf_op jit(solution)/shard_map/ppermute | solution.py:37
  41.5 10.9 %collective-permute-start.1 = (f32[256,320]{0,1:T(8,128)S(1)}, f32[256,320]{0,1:T(8,128)S(1)}, u32[]{:S(2)}, u32[]{:S(2)}) collective-permute-start(f32[256,320]{0,1:T(8,128)S(1)} %collective-permute-done), channel_id=1, source_target_pairs={{0,8},{8,16},{16,24},{24,0},{1,9},{9,17},{17,25},{25,1},{2,10},{10... | collective-permute-start | bytes 983048 | tf_op jit(solution)/shard_map/ppermute | solution.py:37
  52.4 10.1 %collective-permute-start.2 = (f32[256,320]{0,1:T(8,128)S(1)}, f32[256,320]{0,1:T(8,128)S(1)}, u32[]{:S(2)}, u32[]{:S(2)}) collective-permute-start(f32[256,320]{0,1:T(8,128)S(1)} %collective-permute-done.1), channel_id=1, source_target_pairs={{0,8},{8,16},{16,24},{24,0},{1,9},{9,17},{17,25},{25,1},{2,10},{10... | collective-permute-start | bytes 983048 | tf_op jit(solution)/shard_map/ppermute | solution.py:37
  75.0 5.1 %copy-start.1 = (f32[128,2304]{1,0:T(8,128)S(1)}, f32[128,2304]{1,0:T(8,128)}, u32[]{:S(2)}) copy-start(f32[128,2304]{1,0:T(8,128)} %param.13) | copy-start | bytes 3538948
Sparse Core Ops, SparseCore 0:
  9.2 33.4 all-gather.1
  83.7 39.5 reduce-scatter.1
